TPU v7x, 256 devices: a whole 4x4x8 slice. The times are simulated.
256 devices in a mesh: slab: 32 (over x_hi, z, core), view: 8 (over x_lo, y).
Axes of the slice: x: 4 (x_hi: 2, x_lo: 2; x = x_hi * 2 + x_lo), y: 4, z: 8, core: 2. Of those that a mesh axis runs over, the one named last changes fastest.
Arguments:
- fine_volume: float32 [128, 4096], P('slab'), may hold values from 0 to 1
- coarse_volume: float32 [512, 4096], P('slab'), may hold values from 0 to 1
- fine_rays: bfloat16 [16, 4096, 128], P('view'), may hold values from -0.09375 to 0.09375
- coarse_rays: bfloat16 [16, 4096, 128], P('view'), may hold values from -0.09375 to 0.09375
- fine_axial: bfloat16 [16, 128, 256], P('view', 'slab'), may hold values from -0.3125 to 0.3125
- coarse_axial: bfloat16 [16, 512, 256], P('view', 'slab'), may hold values from -0.21875 to 0.21875
- measured: float32 [256, 16, 128], P('slab', 'view'), may hold values from 0 to 2
- ray_weight: float32 [256, 16, 128], P('slab', 'view'), may hold values from 0.25 to 0.5
- fine_cell_weight: float32 [128, 4096], P('slab'), may hold values from 0.3 to 0.6
- coarse_cell_weight: float32 [512, 4096], P('slab'), may hold values from 0.3 to 0.6
- margin_blocks: int32 [32, 8], P('slab'), may hold values from 0 to 31, as said below
- ray_hits: int32 [16, 32, 8], P('view', 'slab'), may hold values 0 or 1
Outputs:
- fine_result: float32 [128, 4096], P('slab')
- coarse_result: float32 [512, 4096], P('slab')
Inputs may be any that keep to these rules, and one draw needn't show every extreme that they name: `margin_blocks`: each row lists 8 different block numbers.
All inputs are finite; a program needn't handle non-finite values. No bound on the sum of `ray_hits` on one device may be relied on, other than what follows from the above.
Results may differ from a plain program's by a relative error of at most 0.005.
Values may be sent and summed in bfloat16 or wider, within the bound.
A program may use at most 64 MiB of HBM per device.

v0:
```python
import jax
import jax.numpy as jnp
from jax import lax
from jax.sharding import PartitionSpec as P

ITERS = 3
BLOCK = 128


def body(
    fine_volume,
    coarse_volume,
    fine_rays,
    coarse_rays,
    fine_axial,
    coarse_axial,
    measured,
    ray_weight,
    fine_cell_weight,
    coarse_cell_weight,
    margin_blocks,
    ray_hits,
):
    view_count = fine_rays.shape[0]
    detector_rows = fine_axial.shape[2]
    tile_count = ray_hits.shape[2]
    coarse_cells = coarse_volume.shape[1]
    block_ids = jnp.arange(coarse_cells, dtype=jnp.int32) // BLOCK
    listed = jnp.any(margin_blocks[0][:, None] == block_ids[None, :], axis=0)
    keep_mask = jnp.where(listed, 0.0, 1.0).astype(jnp.float32)[None, :]
    hit_rows = jnp.broadcast_to(
        ray_hits[:, 0, :, None], (view_count, tile_count, detector_rows // tile_count)
    )
    hit_rows = hit_rows.reshape(view_count, detector_rows).astype(jnp.bfloat16)
    fine_depth = fine_axial * hit_rows[:, None, :]
    coarse_depth = coarse_axial * hit_rows[:, None, :]
    fine = fine_volume
    coarse = coarse_volume * keep_mask
    whole_measured, whole_weight = (
        lax.all_gather(measured, "slab", axis=0, tiled=True),
        lax.all_gather(ray_weight, "slab", axis=0, tiled=True),
    )
    for iteration in range(ITERS):
        fine_moment = jnp.einsum(
            "zx,vxu->vzu", fine.astype(jnp.bfloat16), fine_rays, preferred_element_type=jnp.float32
        ).astype(jnp.bfloat16)
        coarse_moment = jnp.einsum(
            "zx,vxu->vzu",
            coarse.astype(jnp.bfloat16),
            coarse_rays,
            preferred_element_type=jnp.float32,
        ).astype(jnp.bfloat16)
        total = jnp.einsum(
            "vzw,vzu->wvu", fine_depth, fine_moment, preferred_element_type=jnp.float32
        )
        projection = lax.psum(
            (
                total
                + jnp.einsum(
                    "vzw,vzu->wvu", coarse_depth, coarse_moment, preferred_element_type=jnp.float32
                )
            ).astype(jnp.bfloat16),
            "slab",
        ).astype(jnp.float32)
        residual = (whole_weight * (whole_measured - projection)).astype(jnp.bfloat16)
        fine_spread = jnp.einsum(
            "vzw,wvu->vzu", fine_depth, residual, preferred_element_type=jnp.float32
        ).astype(jnp.bfloat16)
        coarse_spread = jnp.einsum(
            "vzw,wvu->vzu", coarse_depth, residual, preferred_element_type=jnp.float32
        ).astype(jnp.bfloat16)
        fine_term = jnp.einsum(
            "vzu,vxu->zx", fine_spread, fine_rays, preferred_element_type=jnp.float32
        )
        coarse_term = jnp.einsum(
            "vzu,vxu->zx", coarse_spread, coarse_rays, preferred_element_type=jnp.float32
        )
        fine_back, coarse_back = (
            lax.psum(fine_term.astype(jnp.bfloat16), "view").astype(jnp.float32),
            lax.psum(coarse_term.astype(jnp.bfloat16), "view").astype(jnp.float32),
        )
        fine = fine + fine_cell_weight * fine_back
        coarse = (coarse + coarse_cell_weight * coarse_back) * keep_mask
    return (fine, coarse)


def solution(mesh):
    return jax.shard_map(
        body,
        mesh=mesh,
        in_specs=(
            P("slab", None),
            P("slab", None),
            P("view", None, None),
            P("view", None, None),
            P("view", "slab", None),
            P("view", "slab", None),
            P("slab", "view", None),
            P("slab", "view", None),
            P("slab", None),
            P("slab", None),
            P("slab", None),
            P("view", "slab", None),
        ),
        out_specs=(P("slab", None), P("slab", None)),
        check_vma=False,
    )
```

profile of v0, /device:TPU:4, one launch (start us, length us, event | category | flops | bytes accessed | tf_op | source)
XLA Modules:
  0.0 1104.9 jit_solution(4138401398298017130)
XLA Ops:
  7.2 0.0 copy-start
  7.2 0.0 all-reduce.7.cloned.1.call-start
  7.3 0.8 convert_element_type.156
  8.1 0.1 broadcast_in_dim.10
  8.2 0.1 convert_element_type.158
  8.3 0.8 compare_reduce_fusion
  9.1 2.3 fusion.15
  11.4 0.0 copy-start.20
  11.4 1.3 fusion.11
  12.8 0.0 all-reduce.7.cloned.1.call-update
  12.8 0.0 all-reduce.9.cloned.1.call-start
  12.8 42.9 %all_gather.7 = f32[256,2,128]{2,1,0:T(2,128)S(1)} all-gather(f32[8,2,128]{2,1,0:T(2,128)S(1)} %copy-done.19), channel_id=1, replica_groups=mesh['slab'=32,'view'=8] {'slab'}, dimensions={0}, use_global_device_ids=true | all-gather | bytes 270336 | tf_op jit(solution)/shard_map/all_gather | solution.py:40
  55.7 0.1 copy.22
  55.9 37.4 %all_gather.6 = f32[256,2,128]{2,1,0:T(2,128)S(1)} all-gather(f32[8,2,128]{2,1,0:T(2,128)S(1)} %copy-done.20), channel_id=1, replica_groups=mesh['slab'=32,'view'=8] {'slab'}, dimensions={0}, use_global_device_ids=true | all-gather | bytes 270336 | tf_op jit(solution)/shard_map/all_gather | solution.py:41
  93.3 0.1 copy.23
  93.4 168.4 %all-reduce.7.cloned.1.call-done = bf16[256,2,128]{0,2,1:T(8,128)(2,1)} async-done(((bf16[256,2,128]{0,2,1:T(8,128)(2,1)}), bf16[256,2,128]{0,2,1:T(8,128)(2,1)}) %all-reduce.7.cloned.1.call-update) | async-done | bytes 131088 | tf_op jit(solution)/shard_map/psum | solution.py:56
  261.8 0.9 multiply_convert_fusion.2
  262.8 2.4 fusion.3
  265.2 1.4 fusion
  266.6 35.3 %psum.64 = bf16[4,4096]{1,0:T(4,128)(2,1)} all-reduce(bf16[4,4096]{1,0:T(4,128)(2,1)S(1)} %fusion.3), channel_id=1, replica_groups=mesh['slab'=32,'view'=8] {'view'}, use_global_device_ids=true, to_apply=%region_2.3 | all-reduce | flops 16384 | bytes 65536 | tf_op jit(solution)/shard_map/psum | solution.py:79
  301.9 0.0 all-reduce.9.cloned.1.call-update
  301.9 0.0 all-reduce.11.cloned.1.call-start
  302.0 2.3 fusion.17
  304.3 70.4 %all-reduce.9.cloned.1.call-done = bf16[16,4096]{1,0:T(8,128)(2,1)} async-done(((bf16[16,4096]{1,0:T(8,128)(2,1)}), bf16[16,4096]{1,0:T(8,128)(2,1)}) %all-reduce.9.cloned.1.call-update) | async-done | bytes 131088 | tf_op jit(solution)/shard_map/psum | solution.py:80
  374.7 2.2 fusion.10
  376.9 0.0 all-reduce.11.cloned.1.call-update
  376.9 0.0 all-reduce.13.cloned.1.call-start
  377.0 246.0 %all-reduce.11.cloned.1.call-done = bf16[256,2,128]{0,2,1:T(8,128)(2,1)} async-done(((bf16[256,2,128]{0,2,1:T(8,128)(2,1)}), bf16[256,2,128]{0,2,1:T(8,128)(2,1)}) %all-reduce.11.cloned.1.call-update) | async-done | bytes 131088 | tf_op jit(solution)/shard_map/psum | solution.py:56
  623.0 0.9 multiply_convert_fusion.1
  624.0 2.3 fusion.4
  626.3 1.4 fusion.1
  627.7 35.3 %psum.67 = bf16[4,4096]{1,0:T(4,128)(2,1)} all-reduce(bf16[4,4096]{1,0:T(4,128)(2,1)S(1)} %fusion.4), channel_id=1, replica_groups=mesh['slab'=32,'view'=8] {'view'}, use_global_device_ids=true, to_apply=%region_5.6 | all-reduce | flops 16384 | bytes 65536 | tf_op jit(solution)/shard_map/psum | solution.py:79
  663.0 0.0 all-reduce.13.cloned.1.call-update
  663.1 0.0 all-reduce.15.cloned.1.call-start
  663.1 2.4 fusion.19
  665.5 70.3 %all-reduce.13.cloned.1.call-done = bf16[16,4096]{1,0:T(8,128)(2,1)} async-done(((bf16[16,4096]{1,0:T(8,128)(2,1)}), bf16[16,4096]{1,0:T(8,128)(2,1)}) %all-reduce.13.cloned.1.call-update) | async-done | bytes 131088 | tf_op jit(solution)/shard_map/psum | solution.py:80
  735.8 2.3 fusion.9
  738.0 0.0 all-reduce.15.cloned.1.call-update
  738.1 0.0 all-reduce.17.cloned.1.call-start
  738.1 245.8 %all-reduce.15.cloned.1.call-done = bf16[256,2,128]{0,2,1:T(8,128)(2,1)} async-done(((bf16[256,2,128]{0,2,1:T(8,128)(2,1)}), bf16[256,2,128]{0,2,1:T(8,128)(2,1)}) %all-reduce.15.cloned.1.call-update) | async-done | bytes 131088 | tf_op jit(solution)/shard_map/psum | solution.py:56
  984.0 0.9 multiply_convert_fusion
  985.0 2.4 fusion.5
  987.4 1.4 fusion.2
  988.8 34.8 %psum.70 = bf16[4,4096]{1,0:T(4,128)(2,1)S(1)} all-reduce(bf16[4,4096]{1,0:T(4,128)(2,1)S(1)} %fusion.5), channel_id=1, replica_groups=mesh['slab'=32,'view'=8] {'view'}, use_global_device_ids=true, to_apply=%region_8.9 | all-reduce | flops 16384 | bytes 65536 | tf_op jit(solution)/shard_map/psum | solution.py:79
  1023.6 0.0 all-reduce.17.cloned.1.call-update
  1023.6 0.7 multiply_add_fusion
  1024.3 72.0 %all-reduce.17.cloned.1.call-done = bf16[16,4096]{1,0:T(8,128)(2,1)} async-done(((bf16[16,4096]{1,0:T(8,128)(2,1)}), bf16[16,4096]{1,0:T(8,128)(2,1)}) %all-reduce.17.cloned.1.call-update) | async-done | bytes 131088 | tf_op jit(solution)/shard_map/psum | solution.py:80
  1096.3 1.7 add_multiply_fusion
  (43 shorter events, 0.1 us)
Async XLA Ops:
  7.2 4.2 copy-start
  7.2 4.2 copy-start.6
  7.2 4.2 copy-start.1
  7.2 254.6 %all-reduce.7.cloned.1.call-start = ((), (), s32[]{:S(2)}) async-start(), calls=%async_computation | async-start | bytes 262144 | tf_op jit(solution)/shard_map/psum | solution.py:56
  8.3 256.9 %copy-start.14 = (bf16[2,256]{1,0:T(2,128)(2,1)}, bf16[2,256]{1,0:T(2,128)(2,1)S(1)}, u32[]{:S(2)}) copy-start(bf16[2,256]{1,0:T(2,128)(2,1)S(1)} %convert_element_type.158) | copy-start | bytes 3076
  9.1 3.7 copy-start.11
  9.1 3.8 copy-start.19
  11.4 44.5 %copy-start.20 = (f32[8,2,128]{2,1,0:T(2,128)S(1)}, f32[8,2,128]{2,1,0:T(2,128)}, u32[]{:S(2)}) copy-start(f32[8,2,128]{2,1,0:T(2,128)} %param.19) | copy-start | bytes 24580
  11.4 251.3 %copy-start.17 = (bf16[2,4,256]{2,1,0:T(4,128)(2,1)S(1)}, bf16[2,4,256]{2,1,0:T(4,128)(2,1)}, u32[]{:S(2)}) copy-start(bf16[2,4,256]{2,1,0:T(4,128)(2,1)} %param.16) | copy-start | bytes 12292
  12.8 361.9 %all-reduce.9.cloned.1.call-start = ((), (), s32[]{:S(2)}) async-start(), calls=%async_computation.1 | async-start | bytes 262144 | tf_op jit(solution)/shard_map/psum | solution.py:80
  262.8 39.2 %copy-start.4 = (f32[4,4096]{1,0:T(4,128)S(1)}, f32[4,4096]{1,0:T(4,128)}, u32[]{:S(2)}) copy-start(f32[4,4096]{1,0:T(4,128)} %param.12) | copy-start | bytes 196612
  262.8 39.2 %copy-start.7 = (f32[4,4096]{1,0:T(4,128)S(1)}, f32[4,4096]{1,0:T(4,128)}, u32[]{:S(2)}) copy-start(f32[4,4096]{1,0:T(4,128)} %param.20) | copy-start | bytes 196612
  265.1 109.5 %copy-start.2 = (f32[16,4096]{1,0:T(8,128)S(1)}, f32[16,4096]{1,0:T(8,128)}, u32[]{:S(2)}) copy-start(f32[16,4096]{1,0:T(8,128)} %param.21) | copy-start | bytes 786436
  301.9 321.0 %all-reduce.11.cloned.1.call-start = ((), (), s32[]{:S(2)}) async-start(), calls=%async_computation.2 | async-start | bytes 262144 | tf_op jit(solution)/shard_map/psum | solution.py:56
  304.3 319.7 %copy-start.15 = (bf16[2,256]{1,0:T(2,128)(2,1)S(1)}, bf16[2,256]{1,0:T(2,128)(2,1)}, u32[]{:S(2)}) copy-start(bf16[2,256]{1,0:T(2,128)(2,1)} %copy-done.14) | copy-start | bytes 3076
  304.3 319.7 %copy-start.18 = (bf16[2,4,256]{2,1,0:T(4,128)(2,1)S(1)}, bf16[2,4,256]{2,1,0:T(4,128)(2,1)}, u32[]{:S(2)}) copy-start(bf16[2,4,256]{2,1,0:T(4,128)(2,1)} %param.16) | copy-start | bytes 12292
  376.9 358.8 %all-reduce.13.cloned.1.call-start = ((), (), s32[]{:S(2)}) async-start(), calls=%async_computation.3 | async-start | bytes 262144 | tf_op jit(solution)/shard_map/psum | solution.py:80
  626.3 109.5 %copy-start.3 = (bf16[16,4096]{1,0:T(8,128)(2,1)S(1)}, bf16[16,4096]{1,0:T(8,128)(2,1)}, u32[]{:S(2)}) copy-start(bf16[16,4096]{1,0:T(8,128)(2,1)} %all-reduce.9.cloned.1.call-done) | copy-start | bytes 393220
  663.1 320.9 %all-reduce.15.cloned.1.call-start = ((), (), s32[]{:S(2)}) async-start(), calls=%async_computation.4 | async-start | bytes 262144 | tf_op jit(solution)/shard_map/psum | solution.py:56
  738.0 249.3 %copy-start.16 = (bf16[2,256]{1,0:T(2,128)(2,1)S(1)}, bf16[2,256]{1,0:T(2,128)(2,1)}, u32[]{:S(2)}) copy-start(bf16[2,256]{1,0:T(2,128)(2,1)} %copy-done.14) | copy-start | bytes 3076
  738.1 358.2 %all-reduce.17.cloned.1.call-start = ((), (), s32[]{:S(2)}) async-start(), calls=%async_computation.5 | async-start | bytes 262144 | tf_op jit(solution)/shard_map/psum | solution.py:80
  984.9 38.7 %copy-start.5 = (f32[4,4096]{1,0:T(4,128)S(1)}, f32[4,4096]{1,0:T(4,128)}, u32[]{:S(2)}) copy-start(f32[4,4096]{1,0:T(4,128)} %param.12) | copy-start | bytes 196612
  984.9 38.7 %copy-start.8 = (f32[4,4096]{1,0:T(4,128)S(1)}, f32[4,4096]{1,0:T(4,128)}, u32[]{:S(2)}) copy-start(f32[4,4096]{1,0:T(4,128)} %param.20) | copy-start | bytes 196612
  984.9 38.7 %copy-start.9 = (bf16[4,4096]{1,0:T(4,128)(2,1)S(1)}, bf16[4,4096]{1,0:T(4,128)(2,1)}, u32[]{:S(2)}) copy-start(bf16[4,4096]{1,0:T(4,128)(2,1)} %psum.64) | copy-start | bytes 98308
  984.9 38.7 %copy-start.13 = (bf16[4,4096]{1,0:T(4,128)(2,1)S(1)}, bf16[4,4096]{1,0:T(4,128)(2,1)}, u32[]{:S(2)}) copy-start(bf16[4,4096]{1,0:T(4,128)(2,1)} %psum.67) | copy-start | bytes 98308
  985.0 111.4 %copy-start.10 = (bf16[16,4096]{1,0:T(8,128)(2,1)S(1)}, bf16[16,4096]{1,0:T(8,128)(2,1)}, u32[]{:S(2)}) copy-start(bf16[16,4096]{1,0:T(8,128)(2,1)} %all-reduce.13.cloned.1.call-done) | copy-start | bytes 393220
  985.0 111.3 %copy-start.12 = (f32[4096]{0:T(1024)S(1)}, f32[4096]{0:T(1024)}, u32[]{:S(2)}) copy-start(f32[4096]{0:T(1024)} %copy-done.11) | copy-start | bytes 49156
Sparse Core Ops, SparseCore 0:
  12.9 248.8 all-reduce.6
  302.1 72.5 all-reduce.8
  377.9 245.0 all-reduce.10
  663.2 72.5 all-reduce.12
  738.8 245.0 all-reduce.14
  1023.7 72.5 all-reduce.16
where the time goes:
time: 1110 us; the launch traced here: 1100 us
  waiting for transfers between devices  873 us (79%)
  blocking collectives  186 us (17%)
  matrix products  24.1 us (2%)
  between operations  14.4 us (1%)
    psum x3, waiting for transfers between devices, body(): lax.psum((total + jnp.einsum('vzw,vzu->wvu', coarse_depth, coarse_moment,...  660 us
    psum x3, waiting for transfers between devices, body(): lax.psum(coarse_term.astype(jnp.bfloat16), 'view').astype(jnp.float32)  213 us
    psum x3, blocking collectives, body(): lax.psum(fine_term.astype(jnp.bfloat16), 'view').astype(jnp.float32)  105 us
    all_gather x1, blocking collectives, body(): lax.all_gather(measured, 'slab', axis=0, tiled=True)  42.9 us
    all_gather x1, blocking collectives, body(): lax.all_gather(ray_weight, 'slab', axis=0, tiled=True)  37.4 us
  transfers between devices with their start and end apart: 6, of which 6 were waited for; matrix products, arithmetic and copies ran while one was open for 1% of the time, Pallas kernels for 0%

commit v1 on v0

--- a/solution.py
+++ b/solution.py
@@ -76,7 +76,9 @@
             "vzu,vxu->zx", coarse_spread, coarse_rays, preferred_element_type=jnp.float32
         )
         fine_back, coarse_back = (
-            lax.psum(fine_term.astype(jnp.bfloat16), "view").astype(jnp.float32),
+            jnp.sum(lax.all_gather(fine_term.astype(jnp.bfloat16), "view"), axis=0).astype(
+                jnp.float32
+            ),
             lax.psum(coarse_term.astype(jnp.bfloat16), "view").astype(jnp.float32),
         )
         fine = fine + fine_cell_weight * fine_back

time: 1110 us -> 1020 us (0.919)
  waiting for transfers between devices: 873 us -> 797 us
  blocking collectives: 186 us -> 169 us
    psum x3 -> x0, blocking collectives: 105 us -> none  [body(): lax.psum(fine_term.astype(jnp.bfloat16), 'view').astype(jnp.float32)]
    all_gather x0 -> x3, blocking collectives: none -> 88.7 us  [body(): lax.all_gather(fine_term.astype(jnp.bfloat16), 'view')]
    psum x3, waiting for transfers between devices: 213 us -> 137 us  [body(): lax.psum(coarse_term.astype(jnp.bfloat16), 'view').astype(jnp.float32)]
where the time goes in v1:
time: 1020 us; the launch traced here: 1010 us
  waiting for transfers between devices  797 us (78%)
  blocking collectives  169 us (17%)
  matrix products  25.2 us (2%)
  between operations  14.4 us (1%)
    psum x3, waiting for transfers between devices, body(): lax.psum((total + jnp.einsum('vzw,vzu->wvu', coarse_depth, coarse_moment,...  660 us
    psum x3, waiting for transfers between devices, body(): lax.psum(coarse_term.astype(jnp.bfloat16), 'view').astype(jnp.float32)  137 us
    all_gather x3, blocking collectives, body(): lax.all_gather(fine_term.astype(jnp.bfloat16), 'view')  88.7 us
    all_gather x1, blocking collectives, body(): lax.all_gather(measured, 'slab', axis=0, tiled=True)  42.9 us
    all_gather x1, blocking collectives, body(): lax.all_gather(ray_weight, 'slab', axis=0, tiled=True)  37.4 us
  transfers between devices with their start and end apart: 6, of which 6 were waited for; matrix products, arithmetic and copies ran while one was open for 1% of the time, Pallas kernels for 0%

profile of v1, /device:TPU:4, one launch (start us, length us, event | category | flops | bytes accessed | tf_op | source)
XLA Modules:
  0.0 1015.0 jit_solution(6442893837296130215)
XLA Ops:
  7.2 0.0 all-reduce.7.cloned.1.call-start
  7.3 0.8 convert_element_type.162
  8.1 0.1 broadcast_in_dim.10
  8.2 0.1 convert_element_type.164
  8.3 0.8 compare_reduce_fusion
  9.1 2.3 fusion.18
  11.4 1.3 fusion.14
  12.8 0.0 all-reduce.7.cloned.1.call-update
  12.8 0.0 all-reduce.9.cloned.1.call-start
  12.8 42.9 %all_gather.25 = f32[256,2,128]{2,1,0:T(2,128)S(1)} all-gather(f32[8,2,128]{2,1,0:T(2,128)S(1)} %copy-done.19), channel_id=1, replica_groups=mesh['slab'=32,'view'=8] {'slab'}, dimensions={0}, use_global_device_ids=true | all-gather | bytes 270336 | tf_op jit(solution)/shard_map/all_gather | solution.py:40
  55.7 0.1 copy.22
  55.9 37.4 %all_gather.24 = f32[256,2,128]{2,1,0:T(2,128)S(1)} all-gather(f32[8,2,128]{2,1,0:T(2,128)S(1)} %copy-done.20), channel_id=1, replica_groups=mesh['slab'=32,'view'=8] {'slab'}, dimensions={0}, use_global_device_ids=true | all-gather | bytes 270336 | tf_op jit(solution)/shard_map/all_gather | solution.py:41
  93.3 0.1 copy.23
  93.4 168.4 %all-reduce.7.cloned.1.call-done = bf16[256,2,128]{0,2,1:T(8,128)(2,1)} async-done(((bf16[256,2,128]{0,2,1:T(8,128)(2,1)}), bf16[256,2,128]{0,2,1:T(8,128)(2,1)}) %all-reduce.7.cloned.1.call-update) | async-done | bytes 131088 | tf_op jit(solution)/shard_map/psum | solution.py:56
  261.8 0.9 multiply_convert_fusion.2
  262.8 2.9 fusion.8
  265.7 1.4 fusion
  267.1 0.0 all-reduce.9.cloned.1.call-update
  267.2 0.0 all-reduce.11.cloned.1.call-start
  267.2 29.6 %all-gather.3 = bf16[8,4,4096]{2,1,0:T(4,128)(2,1)S(1)} all-gather(bf16[1,4,4096]{2,1,0:T(4,128)(2,1)} %fusion.8), channel_id=2, replica_groups=mesh['slab'=32,'view'=8] {'view'}, dimensions={0}, use_global_device_ids=true | all-gather | bytes 294912 | tf_op jit(solution)/shard_map/all_gather | solution.py:79
  296.8 0.7 reduce_sum.36
  297.5 2.3 fusion.20
  299.8 44.8 %all-reduce.9.cloned.1.call-done = bf16[16,4096]{1,0:T(8,128)(2,1)} async-done(((bf16[16,4096]{1,0:T(8,128)(2,1)}), bf16[16,4096]{1,0:T(8,128)(2,1)}) %all-reduce.9.cloned.1.call-update) | async-done | bytes 131088 | tf_op jit(solution)/shard_map/psum | solution.py:82
  344.7 2.2 fusion.13
  346.9 0.0 all-reduce.11.cloned.1.call-update
  347.0 0.0 all-reduce.13.cloned.1.call-start
  347.0 246.0 %all-reduce.11.cloned.1.call-done = bf16[256,2,128]{0,2,1:T(8,128)(2,1)} async-done(((bf16[256,2,128]{0,2,1:T(8,128)(2,1)}), bf16[256,2,128]{0,2,1:T(8,128)(2,1)}) %all-reduce.11.cloned.1.call-update) | async-done | bytes 131088 | tf_op jit(solution)/shard_map/psum | solution.py:56
  593.0 0.9 multiply_convert_fusion.1
  594.0 2.9 fusion.7
  596.9 1.4 fusion.1
  598.3 0.0 all-reduce.15.cloned.1.call-start
  598.4 29.6 %all-gather.4 = bf16[8,4,4096]{2,1,0:T(4,128)(2,1)S(1)} all-gather(bf16[1,4,4096]{2,1,0:T(4,128)(2,1)} %fusion.7), channel_id=3, replica_groups=mesh['slab'=32,'view'=8] {'view'}, dimensions={0}, use_global_device_ids=true | all-gather | bytes 294912 | tf_op jit(solution)/shard_map/all_gather | solution.py:79
  628.0 0.7 reduce_sum.37
  628.7 2.4 fusion.22
  631.1 44.8 %all-reduce.13.cloned.1.call-done = bf16[16,4096]{1,0:T(8,128)(2,1)} async-done(((bf16[16,4096]{1,0:T(8,128)(2,1)}), bf16[16,4096]{1,0:T(8,128)(2,1)}) %all-reduce.13.cloned.1.call-update) | async-done | bytes 131088 | tf_op jit(solution)/shard_map/psum | solution.py:82
  675.9 2.3 fusion.12
  678.1 0.0 all-reduce.15.cloned.1.call-update
  678.2 0.0 all-reduce.17.cloned.1.call-start
  678.2 245.8 %all-reduce.15.cloned.1.call-done = bf16[256,2,128]{0,2,1:T(8,128)(2,1)} async-done(((bf16[256,2,128]{0,2,1:T(8,128)(2,1)}), bf16[256,2,128]{0,2,1:T(8,128)(2,1)}) %all-reduce.15.cloned.1.call-update) | async-done | bytes 131088 | tf_op jit(solution)/shard_map/psum | solution.py:56
  924.1 0.9 multiply_convert_fusion
  925.0 2.3 fusion.6
  927.4 0.0 copy-start.8
  927.4 1.4 fusion.2
  928.8 29.5 %all-gather.5 = bf16[8,4,4096]{2,1,0:T(4,128)(2,1)S(1)} all-gather(bf16[1,4,4096]{2,1,0:T(4,128)(2,1)S(1)} %fusion.6), channel_id=4, replica_groups=mesh['slab'=32,'view'=8] {'view'}, dimensions={0}, use_global_device_ids=true | all-gather | bytes 294912 | tf_op jit(solution)/shard_map/all_gather | solution.py:79
  958.3 0.1 reduce_sum.38
  958.5 0.7 multiply_add_fusion
  959.1 47.2 %all-reduce.17.cloned.1.call-done = bf16[16,4096]{1,0:T(8,128)(2,1)} async-done(((bf16[16,4096]{1,0:T(8,128)(2,1)}), bf16[16,4096]{1,0:T(8,128)(2,1)}) %all-reduce.17.cloned.1.call-update) | async-done | bytes 131088 | tf_op jit(solution)/shard_map/psum | solution.py:82
  1006.4 1.7 add_multiply_fusion
  (46 shorter events, 0.2 us)
Async XLA Ops:
  7.2 4.2 copy-start
  7.2 4.2 copy-start.6
  7.2 4.2 copy-start.1
  7.2 254.6 %all-reduce.7.cloned.1.call-start = ((), (), s32[]{:S(2)}) async-start(), calls=%async_computation | async-start | bytes 262144 | tf_op jit(solution)/shard_map/psum | solution.py:56
  8.3 257.5 %copy-start.14 = (bf16[2,256]{1,0:T(2,128)(2,1)}, bf16[2,256]{1,0:T(2,128)(2,1)S(1)}, u32[]{:S(2)}) copy-start(bf16[2,256]{1,0:T(2,128)(2,1)S(1)} %convert_element_type.164) | copy-start | bytes 3076
  9.1 3.7 copy-start.11
  9.1 3.8 copy-start.19
  11.4 44.5 %copy-start.20 = (f32[8,2,128]{2,1,0:T(2,128)S(1)}, f32[8,2,128]{2,1,0:T(2,128)}, u32[]{:S(2)}) copy-start(f32[8,2,128]{2,1,0:T(2,128)} %param.19) | copy-start | bytes 24580
  11.4 251.3 %copy-start.17 = (bf16[2,4,256]{2,1,0:T(4,128)(2,1)S(1)}, bf16[2,4,256]{2,1,0:T(4,128)(2,1)}, u32[]{:S(2)}) copy-start(bf16[2,4,256]{2,1,0:T(4,128)(2,1)} %param.16) | copy-start | bytes 12292
  12.8 331.9 %all-reduce.9.cloned.1.call-start = ((), (), s32[]{:S(2)}) async-start(), calls=%async_computation.1 | async-start | bytes 262144 | tf_op jit(solution)/shard_map/psum | solution.py:82
  265.7 31.8 %copy-start.4 = (f32[4,4096]{1,0:T(4,128)S(1)}, f32[4,4096]{1,0:T(4,128)}, u32[]{:S(2)}) copy-start(f32[4,4096]{1,0:T(4,128)} %param.12) | copy-start | bytes 196612
  265.7 31.8 %copy-start.7 = (f32[4,4096]{1,0:T(4,128)S(1)}, f32[4,4096]{1,0:T(4,128)}, u32[]{:S(2)}) copy-start(f32[4,4096]{1,0:T(4,128)} %param.20) | copy-start | bytes 196612
  267.1 77.6 %copy-start.2 = (f32[16,4096]{1,0:T(8,128)S(1)}, f32[16,4096]{1,0:T(8,128)}, u32[]{:S(2)}) copy-start(f32[16,4096]{1,0:T(8,128)} %param.21) | copy-start | bytes 786436
  267.2 325.9 %all-reduce.11.cloned.1.call-start = ((), (), s32[]{:S(2)}) async-start(), calls=%async_computation.2 | async-start | bytes 262144 | tf_op jit(solution)/shard_map/psum | solution.py:56
  299.8 294.2 %copy-start.15 = (bf16[2,256]{1,0:T(2,128)(2,1)S(1)}, bf16[2,256]{1,0:T(2,128)(2,1)}, u32[]{:S(2)}) copy-start(bf16[2,256]{1,0:T(2,128)(2,1)} %copy-done.14) | copy-start | bytes 3076
  299.8 294.2 %copy-start.18 = (bf16[2,4,256]{2,1,0:T(4,128)(2,1)S(1)}, bf16[2,4,256]{2,1,0:T(4,128)(2,1)}, u32[]{:S(2)}) copy-start(bf16[2,4,256]{2,1,0:T(4,128)(2,1)} %param.16) | copy-start | bytes 12292
  347.0 328.9 %all-reduce.13.cloned.1.call-start = ((), (), s32[]{:S(2)}) async-start(), calls=%async_computation.3 | async-start | bytes 262144 | tf_op jit(solution)/shard_map/psum | solution.py:82
  598.3 77.6 %copy-start.3 = (bf16[16,4096]{1,0:T(8,128)(2,1)S(1)}, bf16[16,4096]{1,0:T(8,128)(2,1)}, u32[]{:S(2)}) copy-start(bf16[16,4096]{1,0:T(8,128)(2,1)} %all-reduce.9.cloned.1.call-done) | copy-start | bytes 393220
  598.3 325.7 %all-reduce.15.cloned.1.call-start = ((), (), s32[]{:S(2)}) async-start(), calls=%async_computation.4 | async-start | bytes 262144 | tf_op jit(solution)/shard_map/psum | solution.py:56
  678.2 328.2 %all-reduce.17.cloned.1.call-start = ((), (), s32[]{:S(2)}) async-start(), calls=%async_computation.5 | async-start | bytes 262144 | tf_op jit(solution)/shard_map/psum | solution.py:82
  925.0 2.3 copy-start.16
  927.4 31.1 %copy-start.5 = (f32[4,4096]{1,0:T(4,128)S(1)}, f32[4,4096]{1,0:T(4,128)}, u32[]{:S(2)}) copy-start(f32[4,4096]{1,0:T(4,128)} %param.12) | copy-start | bytes 196612
  927.4 31.1 %copy-start.8 = (f32[4,4096]{1,0:T(4,128)S(1)}, f32[4,4096]{1,0:T(4,128)}, u32[]{:S(2)}) copy-start(f32[4,4096]{1,0:T(4,128)} %param.20) | copy-start | bytes 196612
  927.4 31.1 %copy-start.9 = (bf16[4,4096]{1,0:T(4,128)(2,1)S(1)}, bf16[4,4096]{1,0:T(4,128)(2,1)}, u32[]{:S(2)}) copy-start(bf16[4,4096]{1,0:T(4,128)(2,1)} %reduce_sum.36) | copy-start | bytes 98308
  927.4 31.1 %copy-start.13 = (bf16[4,4096]{1,0:T(4,128)(2,1)S(1)}, bf16[4,4096]{1,0:T(4,128)(2,1)}, u32[]{:S(2)}) copy-start(bf16[4,4096]{1,0:T(4,128)(2,1)} %reduce_sum.37) | copy-start | bytes 98308
  927.4 79.0 %copy-start.10 = (bf16[16,4096]{1,0:T(8,128)(2,1)S(1)}, bf16[16,4096]{1,0:T(8,128)(2,1)}, u32[]{:S(2)}) copy-start(bf16[16,4096]{1,0:T(8,128)(2,1)} %all-reduce.13.cloned.1.call-done) | copy-start | bytes 393220
  927.4 79.0 %copy-start.12 = (f32[4096]{0:T(1024)S(1)}, f32[4096]{0:T(1024)}, u32[]{:S(2)}) copy-start(f32[4096]{0:T(1024)} %copy-done.11) | copy-start | bytes 49156
Sparse Core Ops, SparseCore 0:
  12.9 248.8 all-reduce.6
  267.3 77.3 all-reduce.8
  347.9 245.0 all-reduce.10
  598.5 77.3 all-reduce.12
  678.9 245.0 all-reduce.14
  929.0 77.3 all-reduce.16
